TPU v7x, 512 devices: a whole 4x4x16 slice. The times are simulated.
512 devices in a mesh: blk: 8 (over x, z_hi), grp: 64 (over y, z_lo, core).
Axes of the slice: x: 4, y: 4, z: 16 (z_hi: 2, z_lo: 8; z = z_hi * 8 + z_lo), core: 2. Of those that a mesh axis runs over, the one named last changes fastest.
Arguments:
- images: bfloat16 [8192, 1152], P(('blk', 'grp')), may hold values from -6 to 6
- texts: bfloat16 [8192, 1152], P(('blk', 'grp')), may hold values from -6 to 6
- scale: float32 [], replicated, may hold values from 8 to 16
- shift: float32 [], replicated, may hold values from -5 to -3
Outputs:
- image_loss: float32 [8192], P(('blk', 'grp'))
- image_grad: float32 [8192, 1152], P(('blk', 'grp'))
- text_grad: float32 [8192, 1152], P(('blk', 'grp'))
All inputs are finite; a program needn't handle non-finite values.
Results may differ from a plain program's by a relative error of at most 0.0045.
Values may be sent and summed in bfloat16 or wider, within the bound.
A program may use at most 64 MiB of HBM per device.

v0:
```python
import jax
import jax.numpy as jnp
from jax import lax
from jax.sharding import PartitionSpec as P


def unit_rows(values):
    floats = values.astype(jnp.float32)
    norms = jnp.sqrt(jnp.sum(floats * floats, 1, keepdims=True) + 1e-06)
    return (floats / norms, norms)


def back_rows(grads, units, norms):
    return (grads - units * jnp.sum(units * grads, 1, keepdims=True)) / norms


def local(images, texts, scale, shift):
    rows = images.shape[0]
    image_unit, image_norm = unit_rows(images)
    text_unit, text_norm = unit_rows(texts)
    image_emb = image_unit.astype(jnp.bfloat16)
    text_emb = text_unit.astype(jnp.bfloat16)
    groups = lax.axis_size("grp")
    loops = lax.axis_size("blk")
    total = loops * groups * rows
    gathered = lax.all_gather(image_emb, "grp", axis=0, tiled=True)
    seen = lax.all_gather(text_emb, "blk", axis=0, tiled=True)
    place = lax.axis_index("grp")
    here = lax.axis_index("blk")
    image_ids = jnp.arange(groups * rows, dtype=jnp.int32)[:, None]
    column_ids = place * rows + (jnp.arange(loops * rows, dtype=jnp.int32) % rows)[None, :]
    column_blk = (jnp.arange(loops * rows, dtype=jnp.int32) // rows)[None, :]
    label = ((image_ids == column_ids) & (column_blk == here)).astype(jnp.float32)
    logit = (
        scale
        * lax.dot_general(
            gathered, seen, (((1,), (1,)), ((), ())), preferred_element_type=jnp.float32
        )
        + shift
    )
    loss = jnp.sum(jax.nn.softplus(logit * (1.0 - 2.0 * label)), 1) / total
    coef = ((jax.nn.sigmoid(logit) - label) * scale).astype(jnp.bfloat16)
    image_part = jnp.dot(coef, seen, preferred_element_type=jnp.float32)
    text_part = lax.dot_general(
        coef, gathered, (((0,), (0,)), ((), ())), preferred_element_type=jnp.float32
    )
    image_sum = lax.psum_scatter(image_part, "grp", scatter_dimension=0, tiled=True)
    image_loss = lax.psum_scatter(loss, "grp", scatter_dimension=0, tiled=True)
    text_sum = lax.psum_scatter(text_part, "blk", scatter_dimension=0, tiled=True)
    image_grad = back_rows(image_sum, image_unit, image_norm)
    text_grad = back_rows(text_sum, text_unit, text_norm)
    return (image_loss, image_grad, text_grad)


def solution(mesh):
    in_specs = (P(("blk", "grp"), None), P(("blk", "grp"), None), P(), P())
    out_specs = (P(("blk", "grp")), P(("blk", "grp"), None), P(("blk", "grp"), None))
    return jax.shard_map(local, mesh=mesh, in_specs=in_specs, out_specs=out_specs, check_vma=False)
```

profile of v0, /device:TPU:4, one launch (start us, length us, event | category | flops | bytes accessed | tf_op | source)
XLA Modules:
  0.0 706.1 jit_solution(12393039619672209299)
XLA Ops:
  7.2 0.0 all-gather.2.cloned.1.call-start
  7.2 0.9 fusion.3
  8.1 1.5 fusion.7
  9.6 0.0 all-gather.2.cloned.1.call-update
  9.6 0.0 reduce-scatter.5.cloned.1.call-start
  11.0 0.9 fusion.4
  11.9 0.9 fusion.8
  12.7 70.1 %all_gather.7 = bf16[128,1152]{1,0:T(8,128)(2,1)S(1)} all-gather(bf16[16,1152]{1,0:T(8,128)(2,1)S(1)} %fusion.8), channel_id=1, replica_groups=mesh['blk'=8,'grp'=64] {'blk'}, dimensions={0}, use_global_device_ids=true | all-gather | bytes 331776 | tf_op jit(solution)/shard_map/all_gather | solution.py:27
  82.8 59.4 %all-gather.2.cloned.1.call-done = bf16[1024,1152]{1,0:T(8,128)(2,1)} async-done(((bf16[16,1152]{1,0:T(8,128)(2,1)}), bf16[1024,1152]{1,0:T(8,128)(2,1)}) %all-gather.2.cloned.1.call-update) | async-done | bytes 2359312 | tf_op jit(solution)/shard_map/all_gather | solution.py:26
  142.2 3.0 fusion.1
  145.2 0.0 copy-done.2
  145.2 1.5 fusion.9
  146.7 0.0 reduce-scatter.5.cloned.1.call-update
  146.7 0.0 reduce-scatter.3.cloned.1.call-start
  146.8 3.1 fusion.10
  149.9 0.0 reduce-scatter.3.cloned.1.call-update
  149.9 1.3 dynamic-slice
  151.8 216.2 %all-reduce = f32[1024]{0:T(1024)S(1)} all-reduce(f32[1024]{0:T(1024)S(1)} %broadcast_multiply_fusion), channel_id=2, replica_groups=mesh['blk'=8,'grp'=64] {'grp'}, use_global_device_ids=true, to_apply=%region_3.4.clone | all-reduce | flops 1024 | bytes 8192
  368.0 0.6 dynamic-slice.1
  368.6 1.1 multiply_reduce_fusion
  369.6 1.6 subtract_divide_fusion
  371.2 325.6 %reduce-scatter.3.cloned.1.call-done = f32[16,1152]{1,0:T(8,128)} async-done(((f32[1024,1152]{1,0:T(8,128)}), f32[16,1152]{1,0:T(8,128)}) %reduce-scatter.3.cloned.1.call-update) | async-done | bytes 73744 | tf_op jit(solution)/shard_map/reduce_scatter | solution.py:47
  696.9 1.1 multiply_reduce_fusion.1
  698.0 1.6 subtract_divide_fusion.1
  (11 shorter events, 0.0 us)
Async XLA Ops:
  7.2 135.1 %all-gather.2.cloned.1.call-start = ((), (), s32[]{:S(2)}) async-start(), calls=%async_computation.2 | async-start | bytes 2396160 | tf_op jit(solution)/shard_map/all_gather | solution.py:26
  9.6 359.0 %reduce-scatter.5.cloned.1.call-start = ((), (), s32[]{:S(2)}) async-start(), calls=%async_computation.4 | async-start | bytes 663552 | tf_op jit(solution)/shard_map/reduce_scatter | solution.py:49
  142.2 3.0 copy-start.2
  146.7 550.1 %reduce-scatter.3.cloned.1.call-start = ((), (), s32[]{:S(2)}) async-start(), calls=%async_computation.3 | async-start | bytes 4792320 | tf_op jit(solution)/shard_map/reduce_scatter | solution.py:47
  149.9 218.7 %copy-start = (bf16[16,1152]{1,0:T(8,128)(2,1)S(1)}, bf16[16,1152]{1,0:T(8,128)(2,1)}, u32[]{:S(2)}) copy-start(bf16[16,1152]{1,0:T(8,128)(2,1)} %param.5) | copy-start | bytes 110596
  149.9 547.0 %copy-start.1 = (bf16[16,1152]{1,0:T(8,128)(2,1)S(1)}, bf16[16,1152]{1,0:T(8,128)(2,1)}, u32[]{:S(2)}) copy-start(bf16[16,1152]{1,0:T(8,128)(2,1)} %param.4) | copy-start | bytes 110596
Sparse Core Ops, SparseCore 0:
  10.7 131.4 all-gather.1
  146.9 109.8 reduce-scatter.4
  259.6 437.2 reduce-scatter.2
where the time goes:
time: 707 us; the launch traced here: 706 us
  waiting for transfers between devices  385 us (54%)
  blocking collectives  286 us (40%)
  between operations  15.7 us (2%)
  other arithmetic  9.52 us (1%)
  matrix products  7.54 us (1%)
    reduce_scatter x1, waiting for transfers between devices, local(): lax.psum_scatter(image_part, 'grp', scatter_dimension=0, tiled=True)  326 us
    unnamed x1, blocking collectives  216 us
    all_gather x1, blocking collectives, local(): seen = lax.all_gather(text_emb, 'blk', axis=0, tiled=True)  70.1 us
    all_gather x1, waiting for transfers between devices, local(): gathered = lax.all_gather(image_emb, 'grp', axis=0, tiled=True)  59.4 us
  transfers between devices with their start and end apart: 3, of which 2 were waited for; matrix products, arithmetic and copies ran while one was open for 1% of the time, Pallas kernels for 0%

commit v1 on v0

--- a/solution.py
+++ b/solution.py
@@ -23,7 +23,9 @@
     groups = lax.axis_size("grp")
     loops = lax.axis_size("blk")
     total = loops * groups * rows
-    gathered = lax.all_gather(image_emb, "grp", axis=0, tiled=True)
+    gathered = jnp.concatenate(
+        lax.all_to_all(jnp.stack([image_emb] * lax.axis_size("grp")), "grp", 0, 0), axis=0
+    )
     seen = lax.all_gather(text_emb, "blk", axis=0, tiled=True)
     place = lax.axis_index("grp")
     here = lax.axis_index("blk")

time: 707 us -> 755 us (1.068)
  blocking collectives: 286 us -> 340 us
  waiting for transfers between devices: 385 us -> 366 us
  starting transfers between devices: 0.12 us -> 16.4 us
    all_gather x1 -> x0, waiting for transfers between devices: 59.4 us -> none  [local(): gathered = lax.all_gather(image_emb, 'grp', axis=0, tiled=True)]
    all_gather x1, blocking collectives: 70.1 us -> 102 us  [local(): seen = lax.all_gather(text_emb, 'blk', axis=0, tiled=True)]
    reduce_scatter x1, waiting for transfers between devices: 326 us -> 348 us  [local(): lax.psum_scatter(image_part, 'grp', scatter_dimension=0, tiled=True)]
    unnamed x1, blocking collectives: 216 us -> 238 us
    all_to_all x0 -> x1, waiting for transfers between devices: none -> 17.6 us  [local(): lax.all_to_all(jnp.stack([image_emb] * lax.axis_size('grp')), 'grp', 0, 0)]
    all_to_all x0 -> x1, starting transfers between devices: none -> 16.3 us  [local(): lax.all_to_all(jnp.stack([image_emb] * lax.axis_size('grp')), 'grp', 0, 0)]
where the time goes in v1:
time: 755 us; the launch traced here: 754 us
  waiting for transfers between devices  366 us (48%)
  blocking collectives  340 us (45%)
  starting transfers between devices  16.4 us (2%)
  between operations  16 us (2%)
    reduce_scatter x1, waiting for transfers between devices, local(): lax.psum_scatter(image_part, 'grp', scatter_dimension=0, tiled=True)  348 us
    unnamed x1, blocking collectives  238 us
    all_gather x1, blocking collectives, local(): seen = lax.all_gather(text_emb, 'blk', axis=0, tiled=True)  102 us
    all_to_all x1, waiting for transfers between devices, local(): lax.all_to_all(jnp.stack([image_emb] * lax.axis_size('grp')), 'grp', 0, 0)  17.6 us
    all_to_all x1, starting transfers between devices, local(): lax.all_to_all(jnp.stack([image_emb] * lax.axis_size('grp')), 'grp', 0, 0)  16.3 us
  transfers between devices with their start and end apart: 3, of which 2 were waited for; matrix products, arithmetic and copies ran while one was open for 1% of the time, Pallas kernels for 0%

profile of v1, /device:TPU:4, one launch (start us, length us, event | category | flops | bytes accessed | tf_op | source)
XLA Modules:
  0.0 754.4 jit_solution(5277753915352912226)
XLA Ops:
  7.2 0.9 fusion.3
  8.1 0.9 fusion.7
  8.9 1.6 stack.2
  10.5 16.3 %all-to-all-start = ((bf16[64,16,1152]{2,1,0:T(8,128)(2,1)}), bf16[64,16,1152]{2,1,0:T(8,128)(2,1)S(1)}, u32[]{:S(2)}, u32[]{:S(2)}) async-start(bf16[64,16,1152]{2,1,0:T(8,128)(2,1)} %stack.2), calls=%async_computation | async-start | bytes 4718592 | tf_op jit(solution)/shard_map/all_to_all | solution.py:27
  26.8 0.0 reduce-scatter.5.cloned.1.call-start
  28.2 0.0 copy-done
  28.2 0.1 fusion.4
  28.3 0.1 fusion.8
  28.4 101.9 %all_gather.3 = bf16[128,1152]{1,0:T(8,128)(2,1)S(1)} all-gather(bf16[16,1152]{1,0:T(8,128)(2,1)S(1)} %fusion.8), channel_id=1, replica_groups=mesh['blk'=8,'grp'=64] {'blk'}, dimensions={0}, use_global_device_ids=true | all-gather | bytes 331776 | tf_op jit(solution)/shard_map/all_gather | solution.py:29
  130.3 17.6 %all-to-all-done = bf16[64,16,1152]{2,1,0:T(8,128)(2,1)S(1)} async-done(((bf16[64,16,1152]{2,1,0:T(8,128)(2,1)}), bf16[64,16,1152]{2,1,0:T(8,128)(2,1)S(1)}, u32[]{:S(2)}, u32[]{:S(2)}) %all-to-all-start) | async-done | bytes 2359328 | tf_op jit(solution)/shard_map/all_to_all | solution.py:27
  147.9 1.2 fusion.1
  149.1 1.5 fusion.9
  150.5 0.0 reduce-scatter.5.cloned.1.call-update
  150.6 0.0 reduce-scatter.3.cloned.1.call-start
  150.6 3.1 fusion.10
  153.7 0.0 reduce-scatter.3.cloned.1.call-update
  153.7 1.3 dynamic-slice
  155.6 237.8 %all-reduce = f32[1024]{0:T(1024)S(1)} all-reduce(f32[1024]{0:T(1024)S(1)} %broadcast_multiply_fusion), channel_id=2, replica_groups=mesh['blk'=8,'grp'=64] {'grp'}, use_global_device_ids=true, to_apply=%region_3.4.clone | all-reduce | flops 1024 | bytes 8192
  393.5 0.6 dynamic-slice.1
  394.1 1.1 multiply_reduce_fusion
  395.1 1.6 subtract_divide_fusion
  396.8 348.1 %reduce-scatter.3.cloned.1.call-done = f32[16,1152]{1,0:T(8,128)} async-done(((f32[1024,1152]{1,0:T(8,128)}), f32[16,1152]{1,0:T(8,128)}) %reduce-scatter.3.cloned.1.call-update) | async-done | bytes 73744 | tf_op jit(solution)/shard_map/reduce_scatter | solution.py:49
  744.9 1.1 multiply_reduce_fusion.1
  746.0 1.6 subtract_divide_fusion.1
  (9 shorter events, 0.0 us)
Async XLA Ops:
  10.5 17.7 %copy-start = (bf16[16,1152]{1,0:T(8,128)(2,1)S(1)}, bf16[16,1152]{1,0:T(8,128)(2,1)}, u32[]{:S(2)}) copy-start(bf16[16,1152]{1,0:T(8,128)(2,1)} %param.5) | copy-start | bytes 110596
  10.5 137.4 %all-to-all-start = ((bf16[64,16,1152]{2,1,0:T(8,128)(2,1)}), bf16[64,16,1152]{2,1,0:T(8,128)(2,1)S(1)}, u32[]{:S(2)}, u32[]{:S(2)}) async-start(bf16[64,16,1152]{2,1,0:T(8,128)(2,1)} %stack.2), calls=%async_computation | async-start | bytes 4718592 | tf_op jit(solution)/shard_map/all_to_all | solution.py:27
  26.8 367.3 %reduce-scatter.5.cloned.1.call-start = ((), (), s32[]{:S(2)}) async-start(), calls=%async_computation.4 | async-start | bytes 663552 | tf_op jit(solution)/shard_map/reduce_scatter | solution.py:51
  150.6 594.3 %reduce-scatter.3.cloned.1.call-start = ((), (), s32[]{:S(2)}) async-start(), calls=%async_computation.3 | async-start | bytes 4792320 | tf_op jit(solution)/shard_map/reduce_scatter | solution.py:49
  153.7 591.2 %copy-start.1 = (bf16[16,1152]{1,0:T(8,128)(2,1)S(1)}, bf16[16,1152]{1,0:T(8,128)(2,1)}, u32[]{:S(2)}) copy-start(bf16[16,1152]{1,0:T(8,128)(2,1)} %param.4) | copy-start | bytes 110596
Sparse Core Ops, SparseCore 0:
  150.7 153.3 reduce-scatter.4
  306.9 437.9 reduce-scatter.2
